TPU v7x, 256 devices: a whole 4x4x8 slice. The times are simulated.
256 devices in a mesh: dom: 32 (over z, y), batch: 8 (over x, core).
Axes of the slice: x: 4, y: 4, z: 8, core: 2. Of those that a mesh axis runs over, the one named last changes fastest.
Arguments:
- activations: bfloat16 [2048, 65536], P('batch', 'dom'), may hold values from 0 to 2
- tile_weights: bfloat16 [4, 512, 512, 128], P(None, 'dom', 'batch'), may hold values from -0.375 to 0.375
- biases: float32 [4, 65536], P(None, 'dom'), may hold values from -2.5 to 2.5
- source_codes: int32 [4, 512, 4], P(None, 'dom'), may hold values from 0 to 19
- send_list: int32 [4, 32, 4], P(None, 'dom'), may hold values from 0 to 15
Outputs:
- result: bfloat16 [2048, 65536], P('batch', 'dom')
All inputs are finite; a program needn't handle non-finite values.
Results may differ from a plain program's by a relative error of at most 0.0062.
Values may be sent and summed in bfloat16 or wider, within the bound.
A program may use at most 64 MiB of HBM per device.

v0:
```python
import jax
import jax.numpy as jnp
from jax import lax
from jax.sharding import PartitionSpec as P


def body(activations, tile_weights, biases, source_codes, send_list):
    row_count = activations.shape[0]
    tile_width = tile_weights.shape[3]
    block_count = source_codes.shape[1]
    fan_tiles = source_codes.shape[2]
    layer_count = tile_weights.shape[0]
    part_count = lax.axis_size("dom")
    own_index = lax.axis_index("dom")
    neighbor_offsets = (1, 2, -1, part_count // 2)
    offset_table = jnp.array(neighbor_offsets, jnp.int32)
    senders = (own_index - offset_table) % part_count
    destinations = (own_index + offset_table) % part_count
    current = activations.reshape(row_count, block_count, tile_width)
    for layer_index in range(layer_count):
        outgoing = jnp.take(current, send_list[layer_index, 0], axis=1)
        one_hot = (jnp.arange(part_count)[:, None] == destinations[None, :]).astype(jnp.bfloat16)
        out_blocks = jnp.einsum(
            "qn,rnc->qrc", one_hot, outgoing, preferred_element_type=jnp.float32
        ).astype(jnp.bfloat16)
        in_blocks = lax.all_to_all(out_blocks, "dom", split_axis=0, concat_axis=0, tiled=True)
        arrived = jnp.transpose(jnp.take(in_blocks, senders, axis=0), (1, 0, 2))
        block_pool = jnp.concatenate([current, arrived], axis=1)
        input_panel = jnp.take(block_pool, source_codes[layer_index].reshape(-1), axis=1)
        input_panel = input_panel.reshape(row_count, block_count, fan_tiles * tile_width)
        layer_bias = biases[layer_index].reshape(block_count, tile_width)
        summed = jnp.einsum(
            "rjc,jco->rjo",
            input_panel,
            lax.all_gather(tile_weights[layer_index], "batch", axis=1, tiled=True),
            preferred_element_type=jnp.float32,
        )
        current = jnp.maximum(summed + layer_bias[None], 0.0).astype(jnp.bfloat16)
    return current.reshape(row_count, block_count * tile_width)


def solution(mesh):
    in_specs = (
        P("batch", "dom"),
        P(None, "dom", "batch", None),
        P(None, "dom"),
        P(None, "dom", None),
        P(None, "dom", None),
    )
    out_specs = P("batch", "dom")
    return jax.shard_map(body, mesh=mesh, in_specs=in_specs, out_specs=out_specs, check_vma=False)
```

profile of v0, /device:TPU:10, one launch (start us, length us, event | category | flops | bytes accessed | tf_op | source)
XLA Modules:
  0.0 336.6 jit_solution(4580243394682207343)
XLA Ops:
  7.3 1.5 copy.71
  11.0 2.1 copy.74
  13.1 11.9 %all-to-all-start = ((bf16[32,256,128]{2,1,0:T(8,128)(2,1)}), bf16[32,256,128]{2,1,0:T(8,128)(2,1)}, u32[]{:S(2)}, u32[]{:S(2)}) async-start(bf16[32,256,128]{2,1,0:T(8,128)(2,1)} %copy.74), calls=%async_computation | async-start | bytes 4194304 | tf_op jit(solution)/shard_map/all_to_all | solution.py:26
  26.5 47.8 %all-to-all-done = bf16[32,256,128]{2,1,0:T(8,128)(2,1)} async-done(((bf16[32,256,128]{2,1,0:T(8,128)(2,1)}), bf16[32,256,128]{2,1,0:T(8,128)(2,1)}, u32[]{:S(2)}, u32[]{:S(2)}) %all-to-all-start) | async-done | bytes 2097184 | tf_op jit(solution)/shard_map/all_to_all | solution.py:26
  74.3 2.2 gather_fusion.1
  76.7 3.1 gather_fusion.2
  79.8 4.6 %select_bitcast_fusion.3 = bf16[256,64,128]{2,0,1:T(8,128)(2,1)} fusion(bf16[64,256,128]{2,1,0:T(8,128)(2,1)} %gather_fusion.2, pred[64]{0:T(512)(128)(4,1)S(1)} %compare_and_fusion.6), kind=kLoop, calls=%fused_computation.15 | loop fusion | flops 2097152 | bytes 8388672 | tf_op jit(solution)/shard_map/jit(_take)/select_n | solution.py:29
  84.5 6.4 %copy.76 = bf16[256,64,128]{0,2,1:T(8,128)(2,1)} copy(bf16[256,64,128]{2,0,1:T(8,128)(2,1)} %select_bitcast_fusion.3) | data formatting | bytes 8388608 | tf_op jit(solution)/shard_map/jit(_take)/select_n | solution.py:29
  90.8 4.2 %fusion.16 = bf16[256,16,128]{2,0,1:T(8,128)(2,1)S(1)} fusion(bf16[256,16,512]{0,2,1:T(8,128)(2,1)} %bitcast.92, bf16[1,16,512,128]{3,2,1,0:T(8,128)(2,1)} %all-gather.9.cloned.1.call-done, f32[16,128]{1,0:T(8,128)S(1)} %bitcast.101), kind=kOutput, calls=%fused_computation.32 | convolution fusion | flops 538443776 | bytes 7348224 | tf_op jit(solution)/shard_map/rjc,jco->rjo/dot_general | solution.py:32
  96.6 2.2 copy.79
  98.8 6.9 %all-to-all-start.1 = ((bf16[32,256,128]{2,1,0:T(8,128)(2,1)}), bf16[32,256,128]{2,1,0:T(8,128)(2,1)S(1)}, u32[]{:S(2)}, u32[]{:S(2)}) async-start(bf16[32,256,128]{2,1,0:T(8,128)(2,1)} %copy.79), calls=%async_computation.1 | async-start | bytes 4194304 | tf_op jit(solution)/shard_map/all_to_all | solution.py:26
  106.7 47.6 %all-to-all-done.1 = bf16[32,256,128]{2,1,0:T(8,128)(2,1)S(1)} async-done(((bf16[32,256,128]{2,1,0:T(8,128)(2,1)}), bf16[32,256,128]{2,1,0:T(8,128)(2,1)S(1)}, u32[]{:S(2)}, u32[]{:S(2)}) %all-to-all-start.1) | async-done | bytes 2097184 | tf_op jit(solution)/shard_map/all_to_all | solution.py:26
  155.1 3.1 gather_fusion.5
  158.2 4.6 %select_bitcast_fusion.2 = bf16[256,64,128]{2,0,1:T(8,128)(2,1)} fusion(bf16[64,256,128]{2,1,0:T(8,128)(2,1)} %gather_fusion.5, pred[64]{0:T(512)(128)(4,1)S(1)} %compare_and_fusion.4), kind=kLoop, calls=%fused_computation.14 | loop fusion | flops 2097152 | bytes 8388672 | tf_op jit(solution)/shard_map/jit(_take)/select_n | solution.py:29
  162.8 6.4 %copy.80 = bf16[256,64,128]{0,2,1:T(8,128)(2,1)} copy(bf16[256,64,128]{2,0,1:T(8,128)(2,1)} %select_bitcast_fusion.2) | data formatting | bytes 8388608 | tf_op jit(solution)/shard_map/jit(_take)/select_n | solution.py:29
  169.2 4.2 %fusion.19 = bf16[256,16,128]{2,0,1:T(8,128)(2,1)S(1)} fusion(bf16[256,16,512]{0,2,1:T(8,128)(2,1)} %bitcast.93, bf16[1,16,512,128]{3,2,1,0:T(8,128)(2,1)} %all-gather.11.cloned.1.call-done, f32[16,128]{1,0:T(8,128)S(1)} %bitcast.100), kind=kOutput, calls=%fused_computation.33 | convolution fusion | flops 538443776 | bytes 7348224 | tf_op jit(solution)/shard_map/rjc,jco->rjo/dot_general | solution.py:32
  175.0 2.2 copy.83
  177.1 6.6 %all-to-all-start.2 = ((bf16[32,256,128]{2,1,0:T(8,128)(2,1)}), bf16[32,256,128]{2,1,0:T(8,128)(2,1)S(1)}, u32[]{:S(2)}, u32[]{:S(2)}) async-start(bf16[32,256,128]{2,1,0:T(8,128)(2,1)} %copy.83), calls=%async_computation.2 | async-start | bytes 4194304 | tf_op jit(solution)/shard_map/all_to_all | solution.py:26
  184.7 48.1 %all-to-all-done.2 = bf16[32,256,128]{2,1,0:T(8,128)(2,1)S(1)} async-done(((bf16[32,256,128]{2,1,0:T(8,128)(2,1)}), bf16[32,256,128]{2,1,0:T(8,128)(2,1)S(1)}, u32[]{:S(2)}, u32[]{:S(2)}) %all-to-all-start.2) | async-done | bytes 2097184 | tf_op jit(solution)/shard_map/all_to_all | solution.py:26
  233.6 3.1 gather_fusion.8
  236.7 4.6 %select_bitcast_fusion.1 = bf16[256,64,128]{2,0,1:T(8,128)(2,1)} fusion(bf16[64,256,128]{2,1,0:T(8,128)(2,1)} %gather_fusion.8, pred[64]{0:T(512)(128)(4,1)S(1)} %compare_and_fusion.2), kind=kLoop, calls=%fused_computation.13 | loop fusion | flops 2097152 | bytes 8388672 | tf_op jit(solution)/shard_map/jit(_take)/select_n | solution.py:29
  241.3 6.4 %copy.84 = bf16[256,64,128]{0,2,1:T(8,128)(2,1)} copy(bf16[256,64,128]{2,0,1:T(8,128)(2,1)} %select_bitcast_fusion.1) | data formatting | bytes 8388608 | tf_op jit(solution)/shard_map/jit(_take)/select_n | solution.py:29
  247.7 4.2 %fusion.22 = bf16[256,16,128]{2,0,1:T(8,128)(2,1)S(1)} fusion(bf16[256,16,512]{0,2,1:T(8,128)(2,1)} %bitcast.94, bf16[1,16,512,128]{3,2,1,0:T(8,128)(2,1)} %all-gather.13.cloned.1.call-done, f32[16,128]{1,0:T(8,128)S(1)} %bitcast.99), kind=kOutput, calls=%fused_computation.34 | convolution fusion | flops 538443776 | bytes 7348224 | tf_op jit(solution)/shard_map/rjc,jco->rjo/dot_general | solution.py:32
  253.5 2.2 copy.87
  255.6 5.7 %all-to-all-start.3 = ((bf16[32,256,128]{2,1,0:T(8,128)(2,1)}), bf16[32,256,128]{2,1,0:T(8,128)(2,1)S(1)}, u32[]{:S(2)}, u32[]{:S(2)}) async-start(bf16[32,256,128]{2,1,0:T(8,128)(2,1)} %copy.87), calls=%async_computation.3 | async-start | bytes 4194304 | tf_op jit(solution)/shard_map/all_to_all | solution.py:26
  262.8 28.3 %all-gather.15.cloned.1.call-done = bf16[1,16,512,128]{3,1,0,2:T(8,128)(2,1)} async-done(((bf16[1,16,64,128]{3,1,0,2:T(8,128)(2,1)}), bf16[1,16,512,128]{3,1,0,2:T(8,128)(2,1)}) %all-gather.15.cloned.1.call-update) | async-done | bytes 2097168 | tf_op jit(solution)/shard_map/all_gather | solution.py:35
  291.0 4.4 %copy.90 = bf16[1,16,512,128]{2,3,1,0:T(8,128)(2,1)} copy(bf16[1,16,512,128]{3,1,0,2:T(8,128)(2,1)} %all-gather.15.cloned.1.call-done) | data formatting | bytes 4194304 | tf_op jit(solution)/shard_map/all_gather | solution.py:35
  295.4 14.1 %all-to-all-done.3 = bf16[32,256,128]{2,1,0:T(8,128)(2,1)S(1)} async-done(((bf16[32,256,128]{2,1,0:T(8,128)(2,1)}), bf16[32,256,128]{2,1,0:T(8,128)(2,1)S(1)}, u32[]{:S(2)}, u32[]{:S(2)}) %all-to-all-start.3) | async-done | bytes 2097184 | tf_op jit(solution)/shard_map/all_to_all | solution.py:26
  310.3 3.1 gather_fusion.11
  313.4 4.6 %select_bitcast_fusion = bf16[256,64,128]{2,0,1:T(8,128)(2,1)} fusion(bf16[64,256,128]{2,1,0:T(8,128)(2,1)} %gather_fusion.11, pred[64]{0:T(512)(128)(4,1)S(1)} %compare_and_fusion), kind=kLoop, calls=%fused_computation.12 | loop fusion | flops 2097152 | bytes 8388672 | tf_op jit(solution)/shard_map/jit(_take)/select_n | solution.py:29
  318.0 6.5 %copy.88 = bf16[256,64,128]{0,2,1:T(8,128)(2,1)} copy(bf16[256,64,128]{2,0,1:T(8,128)(2,1)} %select_bitcast_fusion) | data formatting | bytes 8388608 | tf_op jit(solution)/shard_map/jit(_take)/select_n | solution.py:29
  324.5 3.6 %fusion.25 = bf16[256,16,128]{2,0,1:T(8,128)(2,1)S(1)} fusion(bf16[256,16,512]{0,2,1:T(8,128)(2,1)} %bitcast.95, bf16[1,16,512,128]{2,3,1,0:T(8,128)(2,1)S(1)} %copy-done, f32[16,128]{1,0:T(8,128)S(1)} %bitcast.98), kind=kOutput, calls=%fused_computation.35 | convolution fusion | flops 538443776 | bytes 7348224 | tf_op jit(solution)/shard_map/rjc,jco->rjo/dot_general | solution.py:32
  (83 shorter events, 16.6 us)
Async XLA Ops:
  8.8 1.4 copy-start.6
  13.1 12.0 %copy-start.1 = (bf16[4,16,64,128]{3,2,1,0:T(8,128)(2,1)S(1)}, bf16[4,16,64,128]{3,2,1,0:T(8,128)(2,1)}, u32[]{:S(2)}) copy-start(bf16[4,16,64,128]{3,2,1,0:T(8,128)(2,1)} %param.13) | copy-start | bytes 3145732
  13.1 61.2 %all-to-all-start = ((bf16[32,256,128]{2,1,0:T(8,128)(2,1)}), bf16[32,256,128]{2,1,0:T(8,128)(2,1)}, u32[]{:S(2)}, u32[]{:S(2)}) async-start(bf16[32,256,128]{2,1,0:T(8,128)(2,1)} %copy.74), calls=%async_computation | async-start | bytes 4194304 | tf_op jit(solution)/shard_map/all_to_all | solution.py:26
  25.0 1.1 copy-start.4
  25.0 1.3 copy-start.5
  25.1 1.4 copy-start.3
  25.1 65.8 %all-gather.9.cloned.1.call-start = ((), (), s32[]{:S(2)}) async-start(), calls=%async_computation.4 | async-start | bytes 2359296 | tf_op jit(solution)/shard_map/all_gather | solution.py:35
  98.8 55.4 %all-to-all-start.1 = ((bf16[32,256,128]{2,1,0:T(8,128)(2,1)}), bf16[32,256,128]{2,1,0:T(8,128)(2,1)S(1)}, u32[]{:S(2)}, u32[]{:S(2)}) async-start(bf16[32,256,128]{2,1,0:T(8,128)(2,1)} %copy.79), calls=%async_computation.1 | async-start | bytes 4194304 | tf_op jit(solution)/shard_map/all_to_all | solution.py:26
  105.7 63.5 %all-gather.11.cloned.1.call-start = ((), (), s32[]{:S(2)}) async-start(), calls=%async_computation.5 | async-start | bytes 2359296 | tf_op jit(solution)/shard_map/all_gather | solution.py:35
  177.1 55.6 %all-to-all-start.2 = ((bf16[32,256,128]{2,1,0:T(8,128)(2,1)}), bf16[32,256,128]{2,1,0:T(8,128)(2,1)S(1)}, u32[]{:S(2)}, u32[]{:S(2)}) async-start(bf16[32,256,128]{2,1,0:T(8,128)(2,1)} %copy.83), calls=%async_computation.2 | async-start | bytes 4194304 | tf_op jit(solution)/shard_map/all_to_all | solution.py:26
  183.7 64.0 %all-gather.13.cloned.1.call-start = ((), (), s32[]{:S(2)}) async-start(), calls=%async_computation.6 | async-start | bytes 2359296 | tf_op jit(solution)/shard_map/all_gather | solution.py:35
  255.6 6.0 %copy-start.2 = (bf16[1,16,64,128]{3,2,1,0:T(8,128)(2,1)S(1)}, bf16[1,16,64,128]{3,2,1,0:T(8,128)(2,1)}, u32[]{:S(2)}) copy-start(bf16[1,16,64,128]{3,2,1,0:T(8,128)(2,1)} %get-tuple-element.18) | copy-start | bytes 786436
  255.6 53.8 %all-to-all-start.3 = ((bf16[32,256,128]{2,1,0:T(8,128)(2,1)}), bf16[32,256,128]{2,1,0:T(8,128)(2,1)S(1)}, u32[]{:S(2)}, u32[]{:S(2)}) async-start(bf16[32,256,128]{2,1,0:T(8,128)(2,1)} %copy.87), calls=%async_computation.3 | async-start | bytes 4194304 | tf_op jit(solution)/shard_map/all_to_all | solution.py:26
  261.4 29.7 %all-gather.15.cloned.1.call-start = ((), (), s32[]{:S(2)}) async-start(), calls=%async_computation.7 | async-start | bytes 2359296 | tf_op jit(solution)/shard_map/all_gather | solution.py:35
  318.0 6.5 %copy-start = (bf16[1,16,512,128]{2,3,1,0:T(8,128)(2,1)S(1)}, bf16[1,16,512,128]{2,3,1,0:T(8,128)(2,1)}, u32[]{:S(2)}) copy-start(bf16[1,16,512,128]{2,3,1,0:T(8,128)(2,1)} %copy.90) | copy-start | bytes 6291460
Sparse Core Ops, SparseCore 0:
  27.7 27.2 all-gather.8
  108.3 27.4 all-gather.10
  186.4 27.2 all-gather.12
  263.7 27.2 all-gather.14
where the time goes:
time: 338 us; the launch traced here: 337 us
  waiting for transfers between devices  187 us (55%)
  local copies, waits for them, and re-layouts  64 us (19%)
  starting transfers between devices  31.6 us (9%)
  other arithmetic  20.6 us (6%)
  matrix products  19.6 us (6%)
  between operations  13.6 us (4%)
    all_to_all x4, waiting for transfers between devices, body(): lax.all_to_all(out_blocks, 'dom', split_axis=0, concat_axis=0, tiled=True)  158 us
    all_to_all x4, starting transfers between devices, body(): lax.all_to_all(out_blocks, 'dom', split_axis=0, concat_axis=0, tiled=True)  31 us
    all_gather x4, waiting for transfers between devices, body(): lax.all_gather(tile_weights[layer_index], 'batch', axis=1, tiled=True)  28.3 us
    select_n x4, local copies, waits for them, and re-layouts, body(): jnp.take(block_pool, source_codes[layer_index].reshape(-1), axis=1)  25.6 us
    select_n x8, other arithmetic, body(): jnp.take(block_pool, source_codes[layer_index].reshape(-1), axis=1)  18.6 us
    dot_general x4, matrix products, body(): jnp.einsum('rjc,jco->rjo', input_panel, lax.all_gather(tile_weights[layer...  16.3 us
    gather x4, local copies, waits for them, and re-layouts, body(): jnp.take(block_pool, source_codes[layer_index].reshape(-1), axis=1)  12.4 us
    convert_element_type x4, local copies, waits for them, and re-layouts, body(): out_blocks = jnp.einsum('qn,rnc->qrc', one_hot, outgoing, preferred_eleme...  8.6 us
  transfers between devices with their start and end apart: 8, of which 5 were waited for; matrix products, arithmetic and copies ran while one was open for 16% of the time, Pallas kernels for 0%

commit v1 on v0

--- a/solution.py
+++ b/solution.py
@@ -2,6 +2,7 @@
 import jax.numpy as jnp
 from jax import lax
 from jax.sharding import PartitionSpec as P
+from jax.lax import all_to_all, axis_size
 
 
 def body(activations, tile_weights, biases, source_codes, send_list):
@@ -29,10 +30,16 @@
         input_panel = jnp.take(block_pool, source_codes[layer_index].reshape(-1), axis=1)
         input_panel = input_panel.reshape(row_count, block_count, fan_tiles * tile_width)
         layer_bias = biases[layer_index].reshape(block_count, tile_width)
+
+        def part_classes(values):
+            return jnp.concatenate(
+                all_to_all(jnp.stack([values for _ in range(axis_size("batch"))]), "batch", 0, 0), 1
+            )
+
         summed = jnp.einsum(
             "rjc,jco->rjo",
             input_panel,
-            lax.all_gather(tile_weights[layer_index], "batch", axis=1, tiled=True),
+            part_classes(tile_weights[layer_index]),
             preferred_element_type=jnp.float32,
         )
         current = jnp.maximum(summed + layer_bias[None], 0.0).astype(jnp.bfloat16)

time: 338 us -> 391 us (1.16)
  waiting for transfers between devices: 187 us -> 213 us
  starting transfers between devices: 31.6 us -> 52 us
  local copies, waits for them, and re-layouts: 64 us -> 82.2 us
  between operations: 13.6 us -> 0.44 us
    all_to_all x4, waiting for transfers between devices: 158 us -> 193 us  [body(): lax.all_to_all(out_blocks, 'dom', split_axis=0, concat_axis=0, tiled=True)]
    all_gather x4 -> x0, waiting for transfers between devices: 28.3 us -> none  [body(): lax.all_gather(tile_weights[layer_index], 'batch', axis=1, tiled=True)]
    all_to_all x0 -> x4, starting transfers between devices: none -> 20.3 us  [part_classes(): all_to_all(jnp.stack([values for _ in range(axis_size('batch'))]), 'batch...]
    all_to_all x0 -> x4, waiting for transfers between devices: none -> 19.3 us  [part_classes(): all_to_all(jnp.stack([values for _ in range(axis_size('batch'))]), 'batch...]
    another operation x0 -> x4, local copies, waits for them, and re-layouts: none -> 7.65 us  [part_classes(): jnp.stack([values for _ in range(axis_size('batch'))])]
    reshape x0 -> x3, local copies, waits for them, and re-layouts: none -> 6.25 us  [part_classes(): jnp.concatenate(all_to_all(jnp.stack([values for _ in range(axis_size('ba...]
    all_gather x1 -> x0, local copies, waits for them, and re-layouts: 4.38 us -> none  [body(): lax.all_gather(tile_weights[layer_index], 'batch', axis=1, tiled=True)]
  transfers between devices with their start and end apart: 8 -> 8, of which waited for: 5 -> 6; matrix products, arithmetic and copies ran while one was open for 16% -> 24% of each run, Pallas kernels for 0% -> 0%
where the time goes in v1:
time: 391 us; the launch traced here: 389 us
  waiting for transfers between devices  213 us (54%)
  local copies, waits for them, and re-layouts  82.2 us (21%)
  starting transfers between devices  52 us (13%)
  other arithmetic  23.3 us (6%)
  matrix products  18.3 us (5%)
    all_to_all x4, waiting for transfers between devices, body(): lax.all_to_all(out_blocks, 'dom', split_axis=0, concat_axis=0, tiled=True)  193 us
    all_to_all x4, starting transfers between devices, body(): lax.all_to_all(out_blocks, 'dom', split_axis=0, concat_axis=0, tiled=True)  31.7 us
    select_n x4, local copies, waits for them, and re-layouts, body(): jnp.take(block_pool, source_codes[layer_index].reshape(-1), axis=1)  26 us
    all_to_all x4, starting transfers between devices, part_classes(): all_to_all(jnp.stack([values for _ in range(axis_size('batch'))]), 'batch...  20.3 us
    all_to_all x4, waiting for transfers between devices, part_classes(): all_to_all(jnp.stack([values for _ in range(axis_size('batch'))]), 'batch...  19.3 us
    select_n x8, other arithmetic, body(): jnp.take(block_pool, source_codes[layer_index].reshape(-1), axis=1)  18.6 us
    dot_general x4, matrix products, body(): jnp.einsum('rjc,jco->rjo', input_panel, part_classes(tile_weights[layer_i...  14.9 us
    gather x4, local copies, waits for them, and re-layouts, body(): jnp.take(block_pool, source_codes[layer_index].reshape(-1), axis=1)  12.4 us
  transfers between devices with their start and end apart: 8, of which 6 were waited for; matrix products, arithmetic and copies ran while one was open for 24% of the time, Pallas kernels for 0%

profile of v1, /device:TPU:10, one launch (start us, length us, event | category | flops | bytes accessed | tf_op | source)
XLA Modules:
  0.0 388.8 jit_solution(12074115498981246567)
XLA Ops:
  4.0 5.0 %all-to-all-start.1 = ((bf16[8,16,64,128]{3,2,1,0:T(8,128)(2,1)}), bf16[8,16,64,128]{3,2,1,0:T(8,128)(2,1)S(1)}, u32[]{:S(2)}, u32[]{:S(2)}) async-start(bf16[8,16,64,128]{3,2,1,0:T(8,128)(2,1)} %stack.12), calls=%async_computation.1 | async-start | bytes 4194304 | tf_op jit(solution)/shard_map/all_to_all | solution.py:36
  15.7 19.0 %all-to-all-done.1 = bf16[8,16,64,128]{3,2,1,0:T(8,128)(2,1)S(1)} async-done(((bf16[8,16,64,128]{3,2,1,0:T(8,128)(2,1)}), bf16[8,16,64,128]{3,2,1,0:T(8,128)(2,1)S(1)}, u32[]{:S(2)}, u32[]{:S(2)}) %all-to-all-start.1) | async-done | bytes 2097184 | tf_op jit(solution)/shard_map/all_to_all | solution.py:36
  34.7 11.8 %all-to-all-start = ((bf16[32,256,128]{2,1,0:T(8,128)(2,1)}), bf16[32,256,128]{2,1,0:T(8,128)(2,1)}, u32[]{:S(2)}, u32[]{:S(2)}) async-start(bf16[32,256,128]{2,1,0:T(8,128)(2,1)} %copy.74), calls=%async_computation | async-start | bytes 4194304 | tf_op jit(solution)/shard_map/all_to_all | solution.py:27
  46.8 48.7 %all-to-all-done = bf16[32,256,128]{2,1,0:T(8,128)(2,1)} async-done(((bf16[32,256,128]{2,1,0:T(8,128)(2,1)}), bf16[32,256,128]{2,1,0:T(8,128)(2,1)}, u32[]{:S(2)}, u32[]{:S(2)}) %all-to-all-start) | async-done | bytes 2097184 | tf_op jit(solution)/shard_map/all_to_all | solution.py:27
  97.3 5.7 %all-to-all-start.3 = ((bf16[8,16,64,128]{3,2,1,0:T(8,128)(2,1)}), bf16[8,16,64,128]{3,2,1,0:T(8,128)(2,1)}, u32[]{:S(2)}, u32[]{:S(2)}) async-start(bf16[8,16,64,128]{3,2,1,0:T(8,128)(2,1)} %stack.13), calls=%async_computation.3 | async-start | bytes 4194304 | tf_op jit(solution)/shard_map/all_to_all | solution.py:36
  104.6 2.2 gather_fusion.1
  107.0 3.1 gather_fusion.2
  110.1 4.6 %select_bitcast_fusion.3 = bf16[256,64,128]{2,0,1:T(8,128)(2,1)} fusion(bf16[64,256,128]{2,1,0:T(8,128)(2,1)} %gather_fusion.2, pred[64]{0:T(512)(128)(4,1)S(1)} %compare_and_fusion.6), kind=kLoop, calls=%fused_computation.15 | loop fusion | flops 2097152 | bytes 8388672 | tf_op jit(solution)/shard_map/jit(_take)/select_n | solution.py:30
  114.8 6.5 %copy.76 = bf16[256,64,128]{0,2,1:T(8,128)(2,1)} copy(bf16[256,64,128]{2,0,1:T(8,128)(2,1)} %select_bitcast_fusion.3) | data formatting | bytes 8388608 | tf_op jit(solution)/shard_map/jit(_take)/select_n | solution.py:30
  121.3 3.6 fusion
  128.9 6.9 %all-to-all-start.2 = ((bf16[32,256,128]{2,1,0:T(8,128)(2,1)}), bf16[32,256,128]{2,1,0:T(8,128)(2,1)S(1)}, u32[]{:S(2)}, u32[]{:S(2)}) async-start(bf16[32,256,128]{2,1,0:T(8,128)(2,1)} %copy.80), calls=%async_computation.2 | async-start | bytes 4194304 | tf_op jit(solution)/shard_map/all_to_all | solution.py:27
  136.0 49.2 %all-to-all-done.2 = bf16[32,256,128]{2,1,0:T(8,128)(2,1)S(1)} async-done(((bf16[32,256,128]{2,1,0:T(8,128)(2,1)}), bf16[32,256,128]{2,1,0:T(8,128)(2,1)S(1)}, u32[]{:S(2)}, u32[]{:S(2)}) %all-to-all-start.2) | async-done | bytes 2097184 | tf_op jit(solution)/shard_map/all_to_all | solution.py:27
  187.2 4.8 %all-to-all-start.5 = ((bf16[8,16,64,128]{3,2,1,0:T(8,128)(2,1)}), bf16[8,16,64,128]{3,2,1,0:T(8,128)(2,1)S(1)}, u32[]{:S(2)}, u32[]{:S(2)}) async-start(bf16[8,16,64,128]{3,2,1,0:T(8,128)(2,1)} %stack.14), calls=%async_computation.5 | async-start | bytes 4194304 | tf_op jit(solution)/shard_map/all_to_all | solution.py:36
  192.0 3.1 copy.82
  198.8 3.1 gather_fusion.5
  201.9 4.6 %select_bitcast_fusion.2 = bf16[256,64,128]{2,0,1:T(8,128)(2,1)} fusion(bf16[64,256,128]{2,1,0:T(8,128)(2,1)} %gather_fusion.5, pred[64]{0:T(512)(128)(4,1)S(1)} %compare_and_fusion.4), kind=kLoop, calls=%fused_computation.14 | loop fusion | flops 2097152 | bytes 8388672 | tf_op jit(solution)/shard_map/jit(_take)/select_n | solution.py:30
  206.5 6.4 %copy.81 = bf16[256,64,128]{0,2,1:T(8,128)(2,1)} copy(bf16[256,64,128]{2,0,1:T(8,128)(2,1)} %select_bitcast_fusion.2) | data formatting | bytes 8388608 | tf_op jit(solution)/shard_map/jit(_take)/select_n | solution.py:30
  212.9 4.2 %fusion.1 = bf16[256,16,128]{2,0,1:T(8,128)(2,1)S(1)} fusion(bf16[256,16,512]{0,2,1:T(8,128)(2,1)} %bitcast.89, bf16[16,512,128]{2,1,0:T(8,128)(2,1)} %bitcast.95, f32[16,128]{1,0:T(8,128)S(1)} %bitcast.99), kind=kOutput, calls=%fused_computation.25 | convolution fusion | flops 538443776 | bytes 7348224 | tf_op jit(solution)/shard_map/rjc,jco->rjo/dot_general | solution.py:39
  222.5 6.8 %all-to-all-start.4 = ((bf16[32,256,128]{2,1,0:T(8,128)(2,1)}), bf16[32,256,128]{2,1,0:T(8,128)(2,1)}, u32[]{:S(2)}, u32[]{:S(2)}) async-start(bf16[32,256,128]{2,1,0:T(8,128)(2,1)} %copy.85), calls=%async_computation.4 | async-start | bytes 4194304 | tf_op jit(solution)/shard_map/all_to_all | solution.py:27
  229.5 49.4 %all-to-all-done.4 = bf16[32,256,128]{2,1,0:T(8,128)(2,1)} async-done(((bf16[32,256,128]{2,1,0:T(8,128)(2,1)}), bf16[32,256,128]{2,1,0:T(8,128)(2,1)}, u32[]{:S(2)}, u32[]{:S(2)}) %all-to-all-start.4) | async-done | bytes 2097184 | tf_op jit(solution)/shard_map/all_to_all | solution.py:27
  280.7 4.8 %all-to-all-start.7 = ((bf16[8,16,64,128]{3,2,1,0:T(8,128)(2,1)}), bf16[8,16,64,128]{3,2,1,0:T(8,128)(2,1)}, u32[]{:S(2)}, u32[]{:S(2)}) async-start(bf16[8,16,64,128]{3,2,1,0:T(8,128)(2,1)} %stack.15), calls=%async_computation.7 | async-start | bytes 4194304 | tf_op jit(solution)/shard_map/all_to_all | solution.py:36
  290.8 3.1 gather_fusion.8
  293.9 4.7 %select_bitcast_fusion.1 = bf16[256,64,128]{2,0,1:T(8,128)(2,1)} fusion(bf16[64,256,128]{2,1,0:T(8,128)(2,1)} %gather_fusion.8, pred[64]{0:T(512)(128)(4,1)S(1)} %compare_and_fusion.2), kind=kLoop, calls=%fused_computation.13 | loop fusion | flops 2097152 | bytes 8388672 | tf_op jit(solution)/shard_map/jit(_take)/select_n | solution.py:30
  298.5 6.5 %copy.86 = bf16[256,64,128]{0,2,1:T(8,128)(2,1)} copy(bf16[256,64,128]{2,0,1:T(8,128)(2,1)} %select_bitcast_fusion.1) | data formatting | bytes 8388608 | tf_op jit(solution)/shard_map/jit(_take)/select_n | solution.py:30
  305.1 3.6 fusion.2
  312.3 6.3 %all-to-all-start.6 = ((bf16[32,256,128]{2,1,0:T(8,128)(2,1)}), bf16[32,256,128]{2,1,0:T(8,128)(2,1)S(1)}, u32[]{:S(2)}, u32[]{:S(2)}) async-start(bf16[32,256,128]{2,1,0:T(8,128)(2,1)} %copy.90), calls=%async_computation.6 | async-start | bytes 4194304 | tf_op jit(solution)/shard_map/all_to_all | solution.py:27
  318.9 3.2 copy.92
  322.1 46.1 %all-to-all-done.6 = bf16[32,256,128]{2,1,0:T(8,128)(2,1)S(1)} async-done(((bf16[32,256,128]{2,1,0:T(8,128)(2,1)}), bf16[32,256,128]{2,1,0:T(8,128)(2,1)S(1)}, u32[]{:S(2)}, u32[]{:S(2)}) %all-to-all-start.6) | async-done | bytes 2097184 | tf_op jit(solution)/shard_map/all_to_all | solution.py:27
  369.0 3.1 gather_fusion.11
  372.1 4.6 %select_bitcast_fusion = bf16[256,64,128]{2,0,1:T(8,128)(2,1)} fusion(bf16[64,256,128]{2,1,0:T(8,128)(2,1)} %gather_fusion.11, pred[64]{0:T(512)(128)(4,1)S(1)} %compare_and_fusion), kind=kLoop, calls=%fused_computation.12 | loop fusion | flops 2097152 | bytes 8388672 | tf_op jit(solution)/shard_map/jit(_take)/select_n | solution.py:30
  376.7 6.5 %copy.91 = bf16[256,64,128]{0,2,1:T(8,128)(2,1)} copy(bf16[256,64,128]{2,0,1:T(8,128)(2,1)} %select_bitcast_fusion) | data formatting | bytes 8388608 | tf_op jit(solution)/shard_map/jit(_take)/select_n | solution.py:30
  383.3 3.6 fusion.3
  (99 shorter events, 43.6 us)
Async XLA Ops:
  4.0 5.0 %copy-start.6 = (bf16[256,2048]{1,0:T(8,128)(2,1)S(1)}, bf16[256,2048]{1,0:T(8,128)(2,1)}, u32[]{:S(2)}) copy-start(bf16[256,2048]{1,0:T(8,128)(2,1)} %param.12) | copy-start | bytes 3145732
  4.0 30.7 %all-to-all-start.1 = ((bf16[8,16,64,128]{3,2,1,0:T(8,128)(2,1)}), bf16[8,16,64,128]{3,2,1,0:T(8,128)(2,1)S(1)}, u32[]{:S(2)}, u32[]{:S(2)}) async-start(bf16[8,16,64,128]{3,2,1,0:T(8,128)(2,1)} %stack.12), calls=%async_computation.1 | async-start | bytes 4194304 | tf_op jit(solution)/shard_map/all_to_all | solution.py:36
  9.0 2.9 copy-start.12
  9.0 3.6 copy-start.14
  15.7 30.8 %copy-start.11 = (s32[4,16,4]{1,2,0:T(4,128)S(1)}, s32[4,16,4]{1,2,0:T(4,128)}, u32[]{:S(2)}) copy-start(s32[4,16,4]{1,2,0:T(4,128)} %param.15) | copy-start | bytes 3076
  15.7 31.0 %copy-start.13 = (s32[4]{0:T(128)S(1)}, s32[4]{0:T(128)}, u32[]{:S(2)}) copy-start(s32[4]{0:T(128)} %constant.64) | copy-start | bytes 52
  15.7 31.0 %copy-start.10 = (f32[4,2048]{1,0:T(4,128)S(1)}, f32[4,2048]{1,0:T(4,128)}, u32[]{:S(2)}) copy-start(f32[4,2048]{1,0:T(4,128)} %param.14) | copy-start | bytes 98308
  15.7 79.7 %copy-start.9 = (bf16[16,64,128]{2,1,0:T(8,128)(2,1)S(1)}, bf16[16,64,128]{2,1,0:T(8,128)(2,1)}, u32[]{:S(2)}) copy-start(bf16[16,64,128]{2,1,0:T(8,128)(2,1)} %get-tuple-element.19) | copy-start | bytes 786436
  34.7 60.8 %all-to-all-start = ((bf16[32,256,128]{2,1,0:T(8,128)(2,1)}), bf16[32,256,128]{2,1,0:T(8,128)(2,1)}, u32[]{:S(2)}, u32[]{:S(2)}) async-start(bf16[32,256,128]{2,1,0:T(8,128)(2,1)} %copy.74), calls=%async_computation | async-start | bytes 4194304 | tf_op jit(solution)/shard_map/all_to_all | solution.py:27
  97.3 31.6 %all-to-all-start.3 = ((bf16[8,16,64,128]{3,2,1,0:T(8,128)(2,1)}), bf16[8,16,64,128]{3,2,1,0:T(8,128)(2,1)}, u32[]{:S(2)}, u32[]{:S(2)}) async-start(bf16[8,16,64,128]{3,2,1,0:T(8,128)(2,1)} %stack.13), calls=%async_computation.3 | async-start | bytes 4194304 | tf_op jit(solution)/shard_map/all_to_all | solution.py:36
  114.8 6.5 %copy-start.2 = (bf16[16,8,64,128]{3,2,1,0:T(8,128)(2,1)S(1)}, bf16[16,8,64,128]{3,2,1,0:T(8,128)(2,1)}, u32[]{:S(2)}) copy-start(bf16[16,8,64,128]{3,2,1,0:T(8,128)(2,1)} %copy.77) | copy-start | bytes 6291460
  124.9 3.7 copy-start.4
  128.6 56.6 %copy-start.8 = (bf16[16,64,128]{2,1,0:T(8,128)(2,1)S(1)}, bf16[16,64,128]{2,1,0:T(8,128)(2,1)}, u32[]{:S(2)}) copy-start(bf16[16,64,128]{2,1,0:T(8,128)(2,1)} %get-tuple-element.21) | copy-start | bytes 786436
  128.9 56.3 %all-to-all-start.2 = ((bf16[32,256,128]{2,1,0:T(8,128)(2,1)}), bf16[32,256,128]{2,1,0:T(8,128)(2,1)S(1)}, u32[]{:S(2)}, u32[]{:S(2)}) async-start(bf16[32,256,128]{2,1,0:T(8,128)(2,1)} %copy.80), calls=%async_computation.2 | async-start | bytes 4194304 | tf_op jit(solution)/shard_map/all_to_all | solution.py:27
  185.1 2.0 copy-start
  187.2 35.4 %all-to-all-start.5 = ((bf16[8,16,64,128]{3,2,1,0:T(8,128)(2,1)}), bf16[8,16,64,128]{3,2,1,0:T(8,128)(2,1)S(1)}, u32[]{:S(2)}, u32[]{:S(2)}) async-start(bf16[8,16,64,128]{3,2,1,0:T(8,128)(2,1)} %stack.14), calls=%async_computation.5 | async-start | bytes 4194304 | tf_op jit(solution)/shard_map/all_to_all | solution.py:36
  217.2 5.4 %copy-start.5 = (bf16[256,16,128]{2,0,1:T(8,128)(2,1)}, bf16[256,16,128]{2,0,1:T(8,128)(2,1)S(1)}, u32[]{:S(2)}) copy-start(bf16[256,16,128]{2,0,1:T(8,128)(2,1)S(1)} %fusion.1) | copy-start | bytes 3145732
  222.5 56.3 %copy-start.7 = (bf16[16,64,128]{2,1,0:T(8,128)(2,1)S(1)}, bf16[16,64,128]{2,1,0:T(8,128)(2,1)}, u32[]{:S(2)}) copy-start(bf16[16,64,128]{2,1,0:T(8,128)(2,1)} %get-tuple-element.18) | copy-start | bytes 786436
  222.5 56.3 %all-to-all-start.4 = ((bf16[32,256,128]{2,1,0:T(8,128)(2,1)}), bf16[32,256,128]{2,1,0:T(8,128)(2,1)}, u32[]{:S(2)}, u32[]{:S(2)}) async-start(bf16[32,256,128]{2,1,0:T(8,128)(2,1)} %copy.85), calls=%async_computation.4 | async-start | bytes 4194304 | tf_op jit(solution)/shard_map/all_to_all | solution.py:27
  280.7 31.6 %all-to-all-start.7 = ((bf16[8,16,64,128]{3,2,1,0:T(8,128)(2,1)}), bf16[8,16,64,128]{3,2,1,0:T(8,128)(2,1)}, u32[]{:S(2)}, u32[]{:S(2)}) async-start(bf16[8,16,64,128]{3,2,1,0:T(8,128)(2,1)} %stack.15), calls=%async_computation.7 | async-start | bytes 4194304 | tf_op jit(solution)/shard_map/all_to_all | solution.py:36
  298.5 6.5 %copy-start.3 = (bf16[16,8,64,128]{3,2,1,0:T(8,128)(2,1)S(1)}, bf16[16,8,64,128]{3,2,1,0:T(8,128)(2,1)}, u32[]{:S(2)}) copy-start(bf16[16,8,64,128]{3,2,1,0:T(8,128)(2,1)} %copy.87) | copy-start | bytes 6291460
  312.3 55.8 %all-to-all-start.6 = ((bf16[32,256,128]{2,1,0:T(8,128)(2,1)}), bf16[32,256,128]{2,1,0:T(8,128)(2,1)S(1)}, u32[]{:S(2)}, u32[]{:S(2)}) async-start(bf16[32,256,128]{2,1,0:T(8,128)(2,1)} %copy.90), calls=%async_computation.6 | async-start | bytes 4194304 | tf_op jit(solution)/shard_map/all_to_all | solution.py:27
  376.7 6.5 %copy-start.1 = (bf16[8,16,64,128]{3,2,0,1:T(8,128)(2,1)S(1)}, bf16[8,16,64,128]{3,2,0,1:T(8,128)(2,1)}, u32[]{:S(2)}) copy-start(bf16[8,16,64,128]{3,2,0,1:T(8,128)(2,1)} %copy.92) | copy-start | bytes 6291460
